TPU v7x, 32 devices: a whole 2x2x4 slice. The times are simulated.
32 devices in a mesh: blk: 16 (over z, y, x), col: 2 (over core).
Axes of the slice: x: 2, y: 2, z: 4, core: 2. Of those that a mesh axis runs over, the one named last changes fastest.
Arguments:
- queries: bfloat16 [128, 16384], P('blk', 'col'), may hold values from -6 to 6
- factor: bfloat16 [16384, 1024], P('col', 'blk'), may hold values from -0.046875 to 0.046875
- eigenvalues: float32 [1024], replicated, may hold values from 0.05 to 20
- damping: float32 [1], replicated, may hold values from 0.5 to 2
- train_rows: bfloat16 [16384, 16384], P('blk', 'col'), may hold values from -0.046875 to 0.046875
Outputs:
- scores: bfloat16 [128, 16384], P('col', 'blk')
All inputs are finite; a program needn't handle non-finite values.
Results may differ from a plain program's by a relative error of at most 0.0049.
Values may be sent and summed in bfloat16 or wider, within the bound.
A program may use at most 64 MiB of HBM per device.

v0:
```python
import jax
import jax.numpy as jnp
from jax import lax
from jax.sharding import PartitionSpec as P


def per_device(queries, factor, eigenvalues, damping, train_rows):
    damp_value = damping[0]
    weights = eigenvalues / (eigenvalues + damp_value)
    query_part = lax.all_to_all(queries, "blk", split_axis=1, concat_axis=0, tiled=True)
    factor_part = lax.all_to_all(factor, "blk", split_axis=0, concat_axis=1, tiled=True)
    partial_value = jnp.dot(query_part, factor_part, preferred_element_type=jnp.float32)
    coefficient = lax.psum(partial_value, ("blk", "col"))
    scaled = coefficient * weights[None, :]
    correction = jnp.dot(scaled, factor_part.astype(jnp.float32).T, precision=lax.Precision.HIGHEST)
    pre_part = ((query_part.astype(jnp.float32) - correction) / damp_value).astype(jnp.bfloat16)
    pre_all = lax.all_gather(pre_part, "blk", axis=1, tiled=True)
    partial_scores = jnp.einsum(
        "qk,nk->qn", pre_all, train_rows, preferred_element_type=jnp.float32
    )
    scores = lax.psum_scatter(partial_scores, "col", scatter_dimension=0, tiled=True)
    return scores.astype(jnp.bfloat16)


def solution(mesh):
    in_specs = (P("blk", "col"), P("col", "blk"), P(), P(), P("blk", "col"))
    out_specs = P("col", "blk")
    return jax.shard_map(
        per_device, mesh=mesh, in_specs=in_specs, out_specs=out_specs, check_vma=False
    )
```

profile of v0, /device:TPU:0, one launch (start us, length us, event | category | flops | bytes accessed | tf_op | source)
XLA Modules:
  0.0 269.8 jit_solution(12998497539709083565)
XLA Ops:
  6.5 8.3 %all-to-all-start = ((bf16[8,16,512]{2,0,1:T(8,128)(2,1)}), bf16[8,16,512]{2,0,1:T(8,128)(2,1)S(1)}, u32[]{:S(2)}, u32[]{:S(2)}) async-start(bf16[8,16,512]{2,0,1:T(8,128)(2,1)} %bitcast.25), calls=%async_computation | async-start | bytes 262144 | tf_op jit(solution)/shard_map/all_to_all | solution.py:10
  14.9 0.0 all-reduce.2.cloned.1.call-start
  14.9 1.3 copy.10
  16.3 6.4 %all-to-all-done = bf16[8,16,512]{2,0,1:T(8,128)(2,1)S(1)} async-done(((bf16[8,16,512]{2,0,1:T(8,128)(2,1)}), bf16[8,16,512]{2,0,1:T(8,128)(2,1)S(1)}, u32[]{:S(2)}, u32[]{:S(2)}) %all-to-all-start) | async-done | bytes 131104 | tf_op jit(solution)/shard_map/all_to_all | solution.py:10
  22.7 28.3 %all_to_all.38 = bf16[16,512,64]{1,2,0:T(8,128)(2,1)S(1)} all-to-all(bf16[16,512,64]{1,2,0:T(8,128)(2,1)S(1)} %bitcast.21), channel_id=1, replica_groups=mesh['blk'=16,'col'=2] {'blk'}, dimensions={0} | all-to-all | bytes 2097152 | tf_op jit(solution)/shard_map/all_to_all | solution.py:11
  51.0 1.3 fusion.4
  52.3 0.0 all-reduce.2.cloned.1.call-update
  52.3 0.0 all-gather.2.cloned.1.call-start
  53.0 0.7 add_divide_fusion
  53.7 126.2 %all-reduce.2.cloned.1.call-done = f32[128,1024]{1,0:T(8,128)} async-done(((f32[128,1024]{1,0:T(8,128)}), f32[128,1024]{1,0:T(8,128)}) %all-reduce.2.cloned.1.call-update) | async-done | bytes 524304 | tf_op jit(solution)/shard_map/psum | solution.py:13
  179.9 2.3 fusion.1
  182.2 0.0 all-gather.2.cloned.1.call-update
  182.2 0.0 reduce-scatter.2.cloned.1.call-start
  182.2 60.3 %all-gather.2.cloned.1.call-done = bf16[128,8192]{1,0:T(8,128)(2,1)} async-done(((bf16[128,512]{1,0:T(8,128)(2,1)}), bf16[128,8192]{1,0:T(8,128)(2,1)}) %all-gather.2.cloned.1.call-update) | async-done | bytes 2097168 | tf_op jit(solution)/shard_map/all_gather | solution.py:17
  242.5 12.9 %fusion.6 = f32[128,1024]{1,0:T(8,128)} fusion(bf16[128,8192]{1,0:T(8,128)(2,1)} %all-gather.2.cloned.1.call-done, bf16[1024,8192]{1,0:T(8,128)(2,1)} %param.9), kind=kOutput, calls=%fused_computation.9 | convolution fusion | flops 2147483648 | bytes 19398656 | tf_op jit(solution)/shard_map/qk,nk->qn/dot_general | solution.py:18
  255.4 0.0 reduce-scatter.2.cloned.1.call-update
  255.4 6.3 %reduce-scatter.2.cloned.1.call-done = f32[64,1024]{1,0:T(8,128)} async-done(((f32[128,1024]{1,0:T(8,128)}), f32[64,1024]{1,0:T(8,128)}) %reduce-scatter.2.cloned.1.call-update) | async-done | bytes 262160 | tf_op jit(solution)/shard_map/reduce_scatter | solution.py:21
  261.7 1.6 convert_element_type.12
Async XLA Ops:
  6.5 16.1 %all-to-all-start = ((bf16[8,16,512]{2,0,1:T(8,128)(2,1)}), bf16[8,16,512]{2,0,1:T(8,128)(2,1)S(1)}, u32[]{:S(2)}, u32[]{:S(2)}) async-start(bf16[8,16,512]{2,0,1:T(8,128)(2,1)} %bitcast.25), calls=%async_computation | async-start | bytes 262144 | tf_op jit(solution)/shard_map/all_to_all | solution.py:10
  14.9 165.0 %all-reduce.2.cloned.1.call-start = ((), (), s32[]{:S(2)}) async-start(), calls=%async_computation.3 | async-start | bytes 1048576 | tf_op jit(solution)/shard_map/psum | solution.py:13
  52.3 190.2 %all-gather.2.cloned.1.call-start = ((), (), s32[]{:S(2)}) async-start(), calls=%async_computation.4 | async-start | bytes 2228224 | tf_op jit(solution)/shard_map/all_gather | solution.py:17
  182.2 79.5 %reduce-scatter.2.cloned.1.call-start = ((), (), s32[]{:S(2)}) async-start(), calls=%async_computation.5 | async-start | bytes 786432 | tf_op jit(solution)/shard_map/reduce_scatter | solution.py:21
Sparse Core Ops, SparseCore 0:
  52.4 127.3 all-reduce.1
  182.6 59.8 all-gather.1
  255.6 6.0 reduce-scatter.1
where the time goes:
time: 270 us
  waiting for transfers between devices  199 us (74%)
  blocking collectives  28.3 us (10%)
  matrix products  16.4 us (6%)
  between operations  13.8 us (5%)
  starting transfers between devices  8.47 us (3%)
    psum x1, waiting for transfers between devices, per_device(): coefficient = lax.psum(partial_value, ('blk', 'col'))  126 us
    all_gather x1, waiting for transfers between devices, per_device(): pre_all = lax.all_gather(pre_part, 'blk', axis=1, tiled=True)  60.3 us
    all_to_all x1, blocking collectives, per_device(): lax.all_to_all(factor, 'blk', split_axis=0, concat_axis=1, tiled=True)  28.3 us
    dot_general x1, matrix products, per_device(): jnp.einsum('qk,nk->qn', pre_all, train_rows, preferred_element_type=jnp.f...  12.9 us
    all_to_all x1, starting transfers between devices, per_device(): lax.all_to_all(queries, 'blk', split_axis=1, concat_axis=0, tiled=True)  8.34 us
    all_to_all x1, waiting for transfers between devices, per_device(): lax.all_to_all(queries, 'blk', split_axis=1, concat_axis=0, tiled=True)  6.41 us
    reduce_scatter x1, waiting for transfers between devices, per_device(): lax.psum_scatter(partial_scores, 'col', scatter_dimension=0, tiled=True)  6.26 us
  transfers between devices with their start and end apart: 4, of which 4 were waited for; matrix products, arithmetic and copies ran while one was open for 1% of the time, Pallas kernels for 0%

commit v1 on v0

--- a/solution.py
+++ b/solution.py
@@ -10,7 +10,8 @@
     query_part = lax.all_to_all(queries, "blk", split_axis=1, concat_axis=0, tiled=True)
     factor_part = lax.all_to_all(factor, "blk", split_axis=0, concat_axis=1, tiled=True)
     partial_value = jnp.dot(query_part, factor_part, preferred_element_type=jnp.float32)
-    coefficient = lax.psum(partial_value, ("blk", "col"))
+    partial = lax.psum(partial_value, "col")
+    coefficient = lax.psum(partial, "blk")
     scaled = coefficient * weights[None, :]
     correction = jnp.dot(scaled, factor_part.astype(jnp.float32).T, precision=lax.Precision.HIGHEST)
     pre_part = ((query_part.astype(jnp.float32) - correction) / damp_value).astype(jnp.bfloat16)

time: 270 us -> 275 us (1.019)
  waiting for transfers between devices: 199 us -> 204 us
    psum x1 -> x2, waiting for transfers between devices: 126 us -> 131 us  [the longest x1 114 us: per_device(): coefficient = lax.psum(partial, 'blk')]
  transfers between devices with their start and end apart: 4 -> 5, of which waited for: 4 -> 5; matrix products, arithmetic and copies ran while one was open for 1% -> 1% of each run, Pallas kernels for 0% -> 0%
where the time goes in v1:
time: 275 us
  waiting for transfers between devices  204 us (74%)
  blocking collectives  28.3 us (10%)
  matrix products  16.4 us (6%)
  between operations  13.8 us (5%)
  starting transfers between devices  8.5 us (3%)
    psum x1, waiting for transfers between devices, per_device(): coefficient = lax.psum(partial, 'blk')  114 us
    all_gather x1, waiting for transfers between devices, per_device(): pre_all = lax.all_gather(pre_part, 'blk', axis=1, tiled=True)  60.3 us
    all_to_all x1, blocking collectives, per_device(): lax.all_to_all(factor, 'blk', split_axis=0, concat_axis=1, tiled=True)  28.3 us
    psum x1, waiting for transfers between devices, per_device(): partial = lax.psum(partial_value, 'col')  17.1 us
    dot_general x1, matrix products, per_device(): jnp.einsum('qk,nk->qn', pre_all, train_rows, preferred_element_type=jnp.f...  12.9 us
    all_to_all x1, starting transfers between devices, per_device(): lax.all_to_all(queries, 'blk', split_axis=1, concat_axis=0, tiled=True)  8.34 us
    all_to_all x1, waiting for transfers between devices, per_device(): lax.all_to_all(queries, 'blk', split_axis=1, concat_axis=0, tiled=True)  6.41 us
    reduce_scatter x1, waiting for transfers between devices, per_device(): lax.psum_scatter(partial_scores, 'col', scatter_dimension=0, tiled=True)  6.26 us
  transfers between devices with their start and end apart: 5, of which 5 were waited for; matrix products, arithmetic and copies ran while one was open for 1% of the time, Pallas kernels for 0%

profile of v1, /device:TPU:0, one launch (start us, length us, event | category | flops | bytes accessed | tf_op | source)
XLA Modules:
  0.0 274.9 jit_solution(5992573453162692020)
XLA Ops:
  6.5 8.3 %all-to-all-start = ((bf16[8,16,512]{2,0,1:T(8,128)(2,1)}), bf16[8,16,512]{2,0,1:T(8,128)(2,1)S(1)}, u32[]{:S(2)}, u32[]{:S(2)}) async-start(bf16[8,16,512]{2,0,1:T(8,128)(2,1)} %bitcast.25), calls=%async_computation | async-start | bytes 262144 | tf_op jit(solution)/shard_map/all_to_all | solution.py:10
  14.9 0.0 all-reduce.3.cloned.1.call-start
  14.9 1.3 copy.10
  16.3 6.4 %all-to-all-done = bf16[8,16,512]{2,0,1:T(8,128)(2,1)S(1)} async-done(((bf16[8,16,512]{2,0,1:T(8,128)(2,1)}), bf16[8,16,512]{2,0,1:T(8,128)(2,1)S(1)}, u32[]{:S(2)}, u32[]{:S(2)}) %all-to-all-start) | async-done | bytes 131104 | tf_op jit(solution)/shard_map/all_to_all | solution.py:10
  22.7 28.3 %all_to_all.38 = bf16[16,512,64]{1,2,0:T(8,128)(2,1)S(1)} all-to-all(bf16[16,512,64]{1,2,0:T(8,128)(2,1)S(1)} %bitcast.21), channel_id=1, replica_groups=mesh['blk'=16,'col'=2] {'blk'}, dimensions={0} | all-to-all | bytes 2097152 | tf_op jit(solution)/shard_map/all_to_all | solution.py:11
  51.0 1.3 fusion.4
  52.3 0.0 all-reduce.3.cloned.1.call-update
  52.3 0.0 all-reduce.5.cloned.1.call-start
  52.4 17.1 %all-reduce.3.cloned.1.call-done = f32[128,1024]{1,0:T(8,128)} async-done(((f32[128,1024]{1,0:T(8,128)}), f32[128,1024]{1,0:T(8,128)}) %all-reduce.3.cloned.1.call-update) | async-done | bytes 524304 | tf_op jit(solution)/shard_map/psum | solution.py:13
  69.4 0.0 all-reduce.5.cloned.1.call-update
  69.5 0.0 all-gather.2.cloned.1.call-start
  70.2 0.7 add_divide_fusion
  70.9 114.1 %all-reduce.5.cloned.1.call-done = f32[128,1024]{1,0:T(8,128)} async-done(((f32[128,1024]{1,0:T(8,128)}), f32[128,1024]{1,0:T(8,128)}) %all-reduce.5.cloned.1.call-update) | async-done | bytes 524304 | tf_op jit(solution)/shard_map/psum | solution.py:14
  184.9 2.3 fusion.1
  187.2 0.0 all-gather.2.cloned.1.call-update
  187.3 0.0 reduce-scatter.2.cloned.1.call-start
  187.3 60.3 %all-gather.2.cloned.1.call-done = bf16[128,8192]{1,0:T(8,128)(2,1)} async-done(((bf16[128,512]{1,0:T(8,128)(2,1)}), bf16[128,8192]{1,0:T(8,128)(2,1)}) %all-gather.2.cloned.1.call-update) | async-done | bytes 2097168 | tf_op jit(solution)/shard_map/all_gather | solution.py:18
  247.6 12.9 %fusion.6 = f32[128,1024]{1,0:T(8,128)} fusion(bf16[128,8192]{1,0:T(8,128)(2,1)} %all-gather.2.cloned.1.call-done, bf16[1024,8192]{1,0:T(8,128)(2,1)} %param.9), kind=kOutput, calls=%fused_computation.9 | convolution fusion | flops 2147483648 | bytes 19398656 | tf_op jit(solution)/shard_map/qk,nk->qn/dot_general | solution.py:19
  260.5 0.0 reduce-scatter.2.cloned.1.call-update
  260.5 6.3 %reduce-scatter.2.cloned.1.call-done = f32[64,1024]{1,0:T(8,128)} async-done(((f32[128,1024]{1,0:T(8,128)}), f32[64,1024]{1,0:T(8,128)}) %reduce-scatter.2.cloned.1.call-update) | async-done | bytes 262160 | tf_op jit(solution)/shard_map/reduce_scatter | solution.py:22
  266.7 1.6 convert_element_type.12
Async XLA Ops:
  6.5 16.1 %all-to-all-start = ((bf16[8,16,512]{2,0,1:T(8,128)(2,1)}), bf16[8,16,512]{2,0,1:T(8,128)(2,1)S(1)}, u32[]{:S(2)}, u32[]{:S(2)}) async-start(bf16[8,16,512]{2,0,1:T(8,128)(2,1)} %bitcast.25), calls=%async_computation | async-start | bytes 262144 | tf_op jit(solution)/shard_map/all_to_all | solution.py:10
  14.9 54.6 %all-reduce.3.cloned.1.call-start = ((), (), s32[]{:S(2)}) async-start(), calls=%async_computation.3 | async-start | bytes 1048576 | tf_op jit(solution)/shard_map/psum | solution.py:13
  52.3 132.6 %all-reduce.5.cloned.1.call-start = ((), (), s32[]{:S(2)}) async-start(), calls=%async_computation.4 | async-start | bytes 1048576 | tf_op jit(solution)/shard_map/psum | solution.py:14
  69.5 178.1 %all-gather.2.cloned.1.call-start = ((), (), s32[]{:S(2)}) async-start(), calls=%async_computation.5 | async-start | bytes 2228224 | tf_op jit(solution)/shard_map/all_gather | solution.py:18
  187.3 79.5 %reduce-scatter.2.cloned.1.call-start = ((), (), s32[]{:S(2)}) async-start(), calls=%async_computation.6 | async-start | bytes 786432 | tf_op jit(solution)/shard_map/reduce_scatter | solution.py:22
Sparse Core Ops, SparseCore 0:
  52.4 16.9 all-reduce.2
  74.6 110.3 all-reduce.4
  187.7 59.8 all-gather.1
  260.6 6.0 reduce-scatter.1
